TPU v7x, 512 devices: a whole 4x8x8 slice. The times are simulated.
512 devices in a mesh: expert: 32 (over y_lo, z, core), dp: 16 (over y_hi, x).
Axes of the slice: x: 4, y: 8 (y_hi: 4, y_lo: 2; y = y_hi * 2 + y_lo), z: 8, core: 2. Of those that a mesh axis runs over, the one named last changes fastest.
Arguments:
- tokens: bfloat16 [65536, 3584], P(('expert', 'dp')), may hold values from -6 to 6
- expert_ids: int32 [65536, 8], P(('expert', 'dp')), may hold values from 0 to 255, all different within a row
- gate_probs: float32 [65536, 8], P(('expert', 'dp')), may hold values from 0.02 to 0.5
- out_grad: bfloat16 [65536, 3584], P(('expert', 'dp')), may hold values from -6 to 6
- w_gate: bfloat16 [32, 1024, 3584], P('expert', 'dp'), may hold values from -0.09375 to 0.09375
- w_up: bfloat16 [32, 1024, 3584], P('expert', 'dp'), may hold values from -0.09375 to 0.09375
- w_down: bfloat16 [32, 1024, 3584], P('expert', 'dp'), may hold values from -0.1875 to 0.1875
Outputs:
- grad_gate: bfloat16 [32, 1024, 3584], P('expert', 'dp')
- grad_up: bfloat16 [32, 1024, 3584], P('expert', 'dp')
- grad_down: bfloat16 [32, 1024, 3584], P('expert', 'dp')
All inputs are finite; a program needn't handle non-finite values.
Results may differ from a plain program's by a relative error of at most 0.0058.
Values may be sent and summed in bfloat16 or wider, within the bound.
A program may use at most 64 MiB of HBM per device.

v0:
```python
import jax
import jax.numpy as jnp
from jax import lax
from jax.sharding import PartitionSpec as P

CAP = 2


def local_factors(rows_x, rows_dy, weight_gate, weight_up, weight_down):
    contract = (((1,), (1,)), ((), ()))
    gate_pre = lax.dot_general(rows_x, weight_gate, contract, preferred_element_type=jnp.float32)
    up_pre = lax.dot_general(rows_x, weight_up, contract, preferred_element_type=jnp.float32)
    back_grad = lax.dot_general(rows_dy, weight_down, contract, preferred_element_type=jnp.float32)
    sig_gate = jax.nn.sigmoid(gate_pre)
    act_gate = gate_pre * sig_gate
    hidden = (act_gate * up_pre).astype(jnp.bfloat16)
    d_gate = (back_grad * up_pre * sig_gate * (1.0 + gate_pre * (1.0 - sig_gate))).astype(
        jnp.bfloat16
    )
    d_up = (back_grad * act_gate).astype(jnp.bfloat16)
    return (d_gate, d_up, hidden)


def outer_sum(factor, rows):
    return lax.dot_general(
        factor, rows, (((0,), (0,)), ((), ())), preferred_element_type=jnp.float32
    )


def local(tokens, expert_ids, gate_probs, out_grad, w_gate, w_up, w_down):
    n_expert = lax.axis_size("expert")
    experts_all = w_gate.shape[0] * n_expert
    tok_rows, top_count = expert_ids.shape
    feature_count = tokens.shape[1]
    flat_ids = expert_ids.reshape(-1)
    expert_range = jnp.arange(experts_all, dtype=jnp.int32)
    onehot = (flat_ids[:, None] == expert_range[None, :]).astype(jnp.int32)
    before = jnp.cumsum(onehot, axis=0) - onehot
    slot_rank = jnp.sum(before * onehot, axis=1)
    kept_mask = (flat_ids < experts_all) & (slot_rank < CAP)
    slot_index = jnp.where(kept_mask, flat_ids * CAP + slot_rank, -1)
    slot_range = jnp.arange(experts_all * CAP, dtype=jnp.int32)
    matches = (slot_index[None, :] == slot_range[:, None]).astype(jnp.float32)
    matches = matches.reshape(experts_all * CAP, tok_rows, top_count)
    picker = jnp.sum(matches, axis=2).astype(jnp.bfloat16)
    slot_prob = jnp.sum(matches * gate_probs[None, :, :], axis=(1, 2))
    sent_x = jnp.dot(picker, tokens, preferred_element_type=jnp.float32).astype(jnp.bfloat16)
    sent_dy = (
        jnp.dot(picker, out_grad, preferred_element_type=jnp.float32) * slot_prob[:, None]
    ).astype(jnp.bfloat16)
    sent_x = sent_x.reshape(experts_all, CAP, feature_count)
    sent_dy = sent_dy.reshape(experts_all, CAP, feature_count)
    recv_x, recv_dy = (
        lax.all_to_all(sent_x, "expert", split_axis=0, concat_axis=0, tiled=True),
        lax.all_to_all(sent_dy, "expert", split_axis=0, concat_axis=0, tiled=True),
    )
    rows_x = recv_x.reshape(-1, feature_count)
    rows_dy = recv_dy.reshape(-1, feature_count)
    piece_x = lax.all_gather(rows_x, "dp", axis=0, tiled=True)
    piece_dy = lax.all_gather(rows_dy, "dp", axis=0, tiled=True)
    d_gate, d_up, hidden = local_factors(piece_x, piece_dy, w_gate[0], w_up[0], w_down[0])
    term_gate = outer_sum(d_gate, piece_x)
    term_up = outer_sum(d_up, piece_x)
    term_down = outer_sum(hidden, piece_dy)
    return (
        term_gate.astype(jnp.bfloat16)[None],
        term_up.astype(jnp.bfloat16)[None],
        term_down.astype(jnp.bfloat16)[None],
    )


def solution(mesh):
    in_specs = (
        P(("expert", "dp"), None),
        P(("expert", "dp"), None),
        P(("expert", "dp"), None),
        P(("expert", "dp"), None),
        P("expert", "dp", None),
        P("expert", "dp", None),
        P("expert", "dp", None),
    )
    out_specs = (P("expert", "dp", None), P("expert", "dp", None), P("expert", "dp", None))
    return jax.shard_map(local, mesh=mesh, in_specs=in_specs, out_specs=out_specs, check_vma=False)
```

profile of v0, /device:TPU:1, one launch (start us, length us, event | category | flops | bytes accessed | tf_op | source)
XLA Modules:
  0.0 293.1 jit_solution(2632505541616493926)
XLA Ops:
  7.2 0.0 copy-start
  7.2 0.0 all-gather.5.cloned.1.call-start
  7.2 0.9 copy.30
  8.1 0.1 eq.43
  8.2 0.1 eq.39
  8.3 9.0 %reduce-window.6 = s32[32,8,128]{2,1,0:T(8,128)S(1)} reduce-window(s32[32,8,128]{2,1,0:T(8,128)S(1)} %fusion.15, s32[]{:T(128)} %constant.4.clone.1), window={size=1x1x128 pad=0_0x0_0x127_0}, to_apply=%region_0.0 | reduce-window | flops 4161536 | bytes 262148 | tf_op jit(solution)/shard_map/reduce-window
  17.3 0.1 slice.8
  17.4 0.1 copy.32
  17.6 0.1 copy.33
  17.7 0.1 broadcast_add_fusion
  17.8 0.1 reduce_sum.30
  18.0 0.7 add_select_fusion
  18.7 1.2 select_reduce_fusion
  19.9 0.3 convolution_convert_fusion.3
  20.2 0.2 reshape.64
  20.4 27.1 %all_to_all.10 = bf16[32,2,3584]{2,1,0:T(2,128)(2,1)S(1)} all-to-all(bf16[32,2,3584]{2,1,0:T(2,128)(2,1)S(1)} %reshape.64), channel_id=1, replica_groups=mesh['expert'=32,'dp'=16] {'expert'}, dimensions={0} | all-to-all | bytes 917504 | tf_op jit(solution)/shard_map/all_to_all | solution.py:54
  47.5 0.9 reshape.65
  48.4 0.0 all-gather.5.cloned.1.call-update
  48.4 0.0 all-gather.3.cloned.1.call-start
  48.5 1.5 fusion
  49.9 0.2 reshape.62
  50.1 19.5 %all_to_all.11 = bf16[32,2,3584]{2,1,0:T(2,128)(2,1)S(1)} all-to-all(bf16[32,2,3584]{2,1,0:T(2,128)(2,1)S(1)} %reshape.62), channel_id=1, replica_groups=mesh['expert'=32,'dp'=16] {'expert'}, dimensions={0} | all-to-all | bytes 917504 | tf_op jit(solution)/shard_map/all_to_all | solution.py:55
  69.6 0.9 reshape.63
  70.6 0.0 all-gather.3.cloned.1.call-update
  70.6 85.9 %all-gather.5.cloned.1.call-done = bf16[1024,3584]{1,0:T(8,128)(2,1)} async-done(((bf16[64,3584]{1,0:T(8,128)(2,1)}), bf16[1024,3584]{1,0:T(8,128)(2,1)}) %all-gather.5.cloned.1.call-update) | async-done | bytes 7340048 | tf_op jit(solution)/shard_map/all_gather | solution.py:59
  156.5 5.5 %fusion.4 = f32[1024,64]{0,1:T(8,128)S(1)} fusion(bf16[1024,3584]{1,0:T(8,128)(2,1)} %all-gather.5.cloned.1.call-done, bf16[1,64,3584]{2,1,0:T(8,128)(2,1)S(1)} %copy-done.3), kind=kOutput, calls=%fused_computation.9 | convolution fusion | flops 469762048 | bytes 8060928 | tf_op jit(solution)/shard_map/dot_general | solution.py:11
  162.1 2.3 fusion.6
  164.4 106.6 %all-gather.3.cloned.1.call-done = bf16[1024,3584]{1,0:T(8,128)(2,1)} async-done(((bf16[64,3584]{1,0:T(8,128)(2,1)}), bf16[1024,3584]{1,0:T(8,128)(2,1)}) %all-gather.3.cloned.1.call-update) | async-done | bytes 7340048 | tf_op jit(solution)/shard_map/all_gather | solution.py:60
  271.0 5.5 %fusion.8 = f32[1024,64]{0,1:T(8,128)S(1)} fusion(bf16[1024,3584]{1,0:T(8,128)(2,1)} %all-gather.3.cloned.1.call-done, bf16[1,64,3584]{2,1,0:T(8,128)(2,1)S(1)} %copy-done.5), kind=kOutput, calls=%fused_computation.13 | convolution fusion | flops 469762048 | bytes 8060928 | tf_op jit(solution)/shard_map/dot_general | solution.py:13
  276.6 2.1 fusion.3
  278.7 5.4 %fusion.1 = bf16[1,64,3584]{2,1,0:T(8,128)(2,1)} fusion(bf16[1024,3584]{1,0:T(8,128)(2,1)} %all-gather.5.cloned.1.call-done, f32[1024,64]{0,1:T(8,128)S(1)} %fusion.4, f32[1024,64]{0,1:T(8,128)S(1)} %fusion.8, f32[1024,64]{0,1:T(8,128)S(1)} %fusion.6), kind=kOutput, calls=%fused_computation.6 | convolution fusion | flops 470646784 | bytes 8585216 | tf_op jit(solution)/shard_map/dot_general | solution.py:25
  284.1 2.1 fusion.2
  (21 shorter events, 0.2 us)
Async XLA Ops:
  7.2 12.8 %copy-start = (bf16[128,3584]{1,0:T(8,128)(2,1)S(1)}, bf16[128,3584]{1,0:T(8,128)(2,1)}, u32[]{:S(2)}) copy-start(bf16[128,3584]{1,0:T(8,128)(2,1)} %param.7) | copy-start | bytes 2752516
  7.2 149.3 %copy-start.3 = (bf16[1,64,3584]{2,1,0:T(8,128)(2,1)S(1)}, bf16[1,64,3584]{2,1,0:T(8,128)(2,1)}, u32[]{:S(2)}) copy-start(bf16[1,64,3584]{2,1,0:T(8,128)(2,1)} %param.11) | copy-start | bytes 1376260
  7.2 149.3 %all-gather.5.cloned.1.call-start = ((), (), s32[]{:S(2)}) async-start(), calls=%async_computation.3 | async-start | bytes 7798784 | tf_op jit(solution)/shard_map/all_gather | solution.py:59
  47.5 114.6 %copy-start.4 = (bf16[1,64,3584]{2,1,0:T(8,128)(2,1)S(1)}, bf16[1,64,3584]{2,1,0:T(8,128)(2,1)}, u32[]{:S(2)}) copy-start(bf16[1,64,3584]{2,1,0:T(8,128)(2,1)} %param.12) | copy-start | bytes 1376260
  48.4 222.6 %all-gather.3.cloned.1.call-start = ((), (), s32[]{:S(2)}) async-start(), calls=%async_computation.2 | async-start | bytes 7798784 | tf_op jit(solution)/shard_map/all_gather | solution.py:60
  70.6 200.4 %copy-start.5 = (bf16[1,64,3584]{2,1,0:T(8,128)(2,1)S(1)}, bf16[1,64,3584]{2,1,0:T(8,128)(2,1)}, u32[]{:S(2)}) copy-start(bf16[1,64,3584]{2,1,0:T(8,128)(2,1)} %param.13) | copy-start | bytes 1376260
  156.5 5.6 %copy-start.1 = (bf16[1024,3584]{1,0:T(8,128)(2,1)S(1)}, bf16[1024,3584]{1,0:T(8,128)(2,1)}, u32[]{:S(2)}) copy-start(bf16[1024,3584]{1,0:T(8,128)(2,1)} %all-gather.5.cloned.1.call-done) | copy-start | bytes 22020100
  271.0 5.5 %copy-start.2 = (bf16[1024,3584]{1,0:T(8,128)(2,1)S(1)}, bf16[1024,3584]{1,0:T(8,128)(2,1)}, u32[]{:S(2)}) copy-start(bf16[1024,3584]{1,0:T(8,128)(2,1)} %all-gather.3.cloned.1.call-done) | copy-start | bytes 22020100
  276.6 7.5 %slice-start = ((s8[7340032]{0:T(1024)(128)(4,1)}), s8[4194304]{0:T(1024)(128)(4,1)S(1)}, s32[]{:S(2)}) async-start(s8[7340032]{0:T(1024)(128)(4,1)} %bitcast.43), calls=%async_computation.4 | async-start | bytes 8388608
  278.7 5.4 %slice-start.1 = ((s8[7340032]{0:T(1024)(128)(4,1)}), s8[3145728]{0:T(1024)(128)(4,1)S(1)}, s32[]{:S(2)}) async-start(s8[7340032]{0:T(1024)(128)(4,1)} %bitcast.43), calls=%async_computation.5 | async-start | bytes 6291456
Sparse Core Ops, SparseCore 0:
  48.6 107.9 all-gather.4
  160.1 110.8 all-gather.2
where the time goes:
time: 293 us
  waiting for transfers between devices  193 us (66%)
  blocking collectives  46.6 us (16%)
  matrix products  24.7 us (8%)
  between operations  14.2 us (5%)
  other arithmetic  11.2 us (4%)
  local copies, waits for them, and re-layouts  3.76 us (1%)
    all_gather x1, waiting for transfers between devices, local(): piece_dy = lax.all_gather(rows_dy, 'dp', axis=0, tiled=True)  107 us
    all_gather x1, waiting for transfers between devices, local(): piece_x = lax.all_gather(rows_x, 'dp', axis=0, tiled=True)  85.9 us
    all_to_all x1, blocking collectives, local(): lax.all_to_all(sent_x, 'expert', split_axis=0, concat_axis=0, tiled=True)  27.1 us
    all_to_all x1, blocking collectives, local(): lax.all_to_all(sent_dy, 'expert', split_axis=0, concat_axis=0, tiled=True)  19.5 us
    dot_general x3, matrix products, outer_sum(): lax.dot_general(factor, rows, (((0,), (0,)), ((), ())), preferred_element...  9.65 us
    another operation x3, other arithmetic  9.15 us
  transfers between devices with their start and end apart: 2, of which 2 were waited for; matrix products, arithmetic and copies ran while one was open for 4% of the time, Pallas kernels for 0%

commit v1 on v0

--- a/solution.py
+++ b/solution.py
@@ -56,8 +56,11 @@
     )
     rows_x = recv_x.reshape(-1, feature_count)
     rows_dy = recv_dy.reshape(-1, feature_count)
-    piece_x = lax.all_gather(rows_x, "dp", axis=0, tiled=True)
-    piece_dy = lax.all_gather(rows_dy, "dp", axis=0, tiled=True)
+    piece_x, piece_dy = jnp.split(
+        lax.all_gather(jnp.concatenate([rows_x, rows_dy], axis=1), "dp", axis=0, tiled=True),
+        [rows_x.shape[1]],
+        axis=1,
+    )
     d_gate, d_up, hidden = local_factors(piece_x, piece_dy, w_gate[0], w_up[0], w_down[0])
     term_gate = outer_sum(d_gate, piece_x)
     term_up = outer_sum(d_up, piece_x)

time: 293 us -> 281 us (0.959)
  blocking collectives: 46.6 us -> 0 us
  starting transfers between devices: 0.08 us -> 18.4 us
  waiting for transfers between devices: 193 us -> 210 us
    all_to_all x2 -> x0, blocking collectives: 46.6 us -> none  [the longest x1 27.1 us: local(): lax.all_to_all(sent_x, 'expert', split_axis=0, concat_axis=0, tiled=True)]
    all_to_all x0 -> x2, waiting for transfers between devices: none -> 26 us  [the longest x1 14.1 us: local(): lax.all_to_all(sent_x, 'expert', split_axis=0, concat_axis=0, tiled=True)]
    all_to_all x0 -> x2, starting transfers between devices: none -> 18.4 us  [the longest x1 13 us: local(): lax.all_to_all(sent_dy, 'expert', split_axis=0, concat_axis=0, tiled=True)]
    all_gather x2 -> x1, waiting for transfers between devices: 193 us -> 184 us  [local(): lax.all_gather(jnp.concatenate([rows_x, rows_dy], axis=1), 'dp', axis=0,...]
    dot_general x1, matrix products: 2.3 us -> 6.1 us  [local_factors(): lax.dot_general(rows_x, weight_up, contract, preferred_element_type=jnp.f...]
    dot_general x3, matrix products: 9.65 us -> 6.47 us  [outer_sum(): lax.dot_general(factor, rows, (((0,), (0,)), ((), ())), preferred_element...]
    dot_general x1, matrix products: 5.53 us -> 2.36 us  [local_factors(): lax.dot_general(rows_dy, weight_down, contract, preferred_element_type=jn...]
  transfers between devices with their start and end apart: 2 -> 3, of which waited for: 2 -> 3; matrix products, arithmetic and copies ran while one was open for 4% -> 1% of each run, Pallas kernels for 0% -> 0%
where the time goes in v1:
time: 281 us; the launch traced here: 280 us
  waiting for transfers between devices  210 us (75%)
  matrix products  22.2 us (8%)
  starting transfers between devices  18.4 us (7%)
  between operations  14.2 us (5%)
  other arithmetic  12.1 us (4%)
  local copies, waits for them, and re-layouts  3.76 us (1%)
    all_gather x1, waiting for transfers between devices, local(): lax.all_gather(jnp.concatenate([rows_x, rows_dy], axis=1), 'dp', axis=0,...  184 us
    all_to_all x1, waiting for transfers between devices, local(): lax.all_to_all(sent_x, 'expert', split_axis=0, concat_axis=0, tiled=True)  14.1 us
    all_to_all x1, starting transfers between devices, local(): lax.all_to_all(sent_dy, 'expert', split_axis=0, concat_axis=0, tiled=True)  13 us
    all_to_all x1, waiting for transfers between devices, local(): lax.all_to_all(sent_dy, 'expert', split_axis=0, concat_axis=0, tiled=True)  11.9 us
    another operation x3, other arithmetic  9.15 us
    dot_general x3, matrix products, outer_sum(): lax.dot_general(factor, rows, (((0,), (0,)), ((), ())), preferred_element...  6.47 us
    dot_general x1, matrix products, local_factors(): lax.dot_general(rows_x, weight_up, contract, preferred_element_type=jnp.f...  6.1 us
  transfers between devices with their start and end apart: 3, of which 3 were waited for; matrix products, arithmetic and copies ran while one was open for 1% of the time, Pallas kernels for 0%

profile of v1, /device:TPU:1, one launch (start us, length us, event | category | flops | bytes accessed | tf_op | source)
XLA Modules:
  0.0 280.4 jit_solution(6570544431004131802)
XLA Ops:
  7.2 0.0 copy-start
  7.2 0.9 copy.30
  8.1 0.1 eq.43
  8.2 0.1 eq.39
  8.3 9.0 %reduce-window.6 = s32[32,8,128]{2,1,0:T(8,128)S(1)} reduce-window(s32[32,8,128]{2,1,0:T(8,128)S(1)} %fusion.39, s32[]{:T(128)} %constant.4.clone.1), window={size=1x1x128 pad=0_0x0_0x127_0}, to_apply=%region_0.0 | reduce-window | flops 4161536 | bytes 262148 | tf_op jit(solution)/shard_map/reduce-window
  17.3 0.1 slice.8
  17.4 0.1 copy.32
  17.6 0.1 copy.33
  17.6 0.1 broadcast_add_fusion
  17.8 0.1 reduce_sum.30
  17.9 0.7 add_select_fusion
  18.7 1.2 convert_reduce_fusion
  19.9 0.3 fusion.21
  20.2 0.9 reshape.64
  21.1 13.0 %all-to-all-start.1 = ((bf16[32,2,3584]{2,1,0:T(2,128)(2,1)}), bf16[32,2,3584]{2,1,0:T(2,128)(2,1)S(1)}, u32[]{:S(2)}, u32[]{:S(2)}) async-start(bf16[32,2,3584]{2,1,0:T(2,128)(2,1)} %reshape.64), calls=%async_computation.1 | async-start | bytes 917504 | tf_op jit(solution)/shard_map/all_to_all | solution.py:55
  34.1 1.4 convolution_convert_fusion
  35.6 0.9 reshape.62
  36.5 11.9 %all-to-all-done.1 = bf16[32,2,3584]{2,1,0:T(2,128)(2,1)S(1)} async-done(((bf16[32,2,3584]{2,1,0:T(2,128)(2,1)}), bf16[32,2,3584]{2,1,0:T(2,128)(2,1)S(1)}, u32[]{:S(2)}, u32[]{:S(2)}) %all-to-all-start.1) | async-done | bytes 458784 | tf_op jit(solution)/shard_map/all_to_all | solution.py:55
  48.4 5.4 %all-to-all-start = ((bf16[32,2,3584]{2,1,0:T(2,128)(2,1)}), bf16[32,2,3584]{2,1,0:T(2,128)(2,1)S(1)}, u32[]{:S(2)}, u32[]{:S(2)}) async-start(bf16[32,2,3584]{2,1,0:T(2,128)(2,1)} %reshape.62), calls=%async_computation | async-start | bytes 917504 | tf_op jit(solution)/shard_map/all_to_all | solution.py:54
  53.8 0.0 all-gather.2.cloned.1.call-start
  53.9 0.2 reshape.65
  54.1 14.1 %all-to-all-done = bf16[32,2,3584]{2,1,0:T(2,128)(2,1)S(1)} async-done(((bf16[32,2,3584]{2,1,0:T(2,128)(2,1)}), bf16[32,2,3584]{2,1,0:T(2,128)(2,1)S(1)}, u32[]{:S(2)}, u32[]{:S(2)}) %all-to-all-start) | async-done | bytes 458784 | tf_op jit(solution)/shard_map/all_to_all | solution.py:54
  68.1 0.2 reshape.63
  68.3 1.0 pad_maximum_fusion
  69.3 0.0 all-gather.2.cloned.1.call-update
  69.3 183.7 %all-gather.2.cloned.1.call-done = bf16[1024,7168]{1,0:T(8,128)(2,1)} async-done(((bf16[64,7168]{1,0:T(8,128)(2,1)}), bf16[1024,7168]{1,0:T(8,128)(2,1)}) %all-gather.2.cloned.1.call-update) | async-done | bytes 14680080 | tf_op jit(solution)/shard_map/all_gather | solution.py:60
  253.1 5.5 %fusion.8 = f32[1024,64]{0,1:T(8,128)S(1)} fusion(bf16[1024,7168]{1,0:T(8,128)(2,1)} %all-gather.2.cloned.1.call-done, bf16[1,64,3584]{2,1,0:T(8,128)(2,1)S(1)} %copy-done.2), kind=kOutput, calls=%fused_computation.8 | convolution fusion | flops 469762048 | bytes 8060928 | tf_op jit(solution)/shard_map/dot_general | solution.py:11
  258.6 6.1 %fusion.10 = f32[1024,64]{0,1:T(8,128)S(1)} fusion(bf16[1024,7168]{1,0:T(8,128)(2,1)} %all-gather.2.cloned.1.call-done, bf16[1,64,3584]{2,1,0:T(8,128)(2,1)S(1)} %copy-done.3), kind=kOutput, calls=%fused_computation.10 | convolution fusion | flops 469762048 | bytes 8060928 | tf_op jit(solution)/shard_map/dot_general | solution.py:12
  264.8 2.4 fusion.2
  267.1 2.2 fusion.25
  269.3 2.2 fusion.28
  271.4 2.1 fusion.22
  (14 shorter events, 0.2 us)
Async XLA Ops:
  7.2 12.7 %copy-start = (bf16[128,3584]{1,0:T(8,128)(2,1)S(1)}, bf16[128,3584]{1,0:T(8,128)(2,1)}, u32[]{:S(2)}) copy-start(bf16[128,3584]{1,0:T(8,128)(2,1)} %param.10) | copy-start | bytes 2752516
  7.2 245.9 %copy-start.2 = (bf16[1,64,3584]{2,1,0:T(8,128)(2,1)S(1)}, bf16[1,64,3584]{2,1,0:T(8,128)(2,1)}, u32[]{:S(2)}) copy-start(bf16[1,64,3584]{2,1,0:T(8,128)(2,1)} %param.11) | copy-start | bytes 1376260
  21.1 27.3 %all-to-all-start.1 = ((bf16[32,2,3584]{2,1,0:T(2,128)(2,1)}), bf16[32,2,3584]{2,1,0:T(2,128)(2,1)S(1)}, u32[]{:S(2)}, u32[]{:S(2)}) async-start(bf16[32,2,3584]{2,1,0:T(2,128)(2,1)} %reshape.64), calls=%async_computation.1 | async-start | bytes 917504 | tf_op jit(solution)/shard_map/all_to_all | solution.py:55
  48.4 19.7 %all-to-all-start = ((bf16[32,2,3584]{2,1,0:T(2,128)(2,1)}), bf16[32,2,3584]{2,1,0:T(2,128)(2,1)S(1)}, u32[]{:S(2)}, u32[]{:S(2)}) async-start(bf16[32,2,3584]{2,1,0:T(2,128)(2,1)} %reshape.62), calls=%async_computation | async-start | bytes 917504 | tf_op jit(solution)/shard_map/all_to_all | solution.py:54
  53.8 199.2 %all-gather.2.cloned.1.call-start = ((), (), s32[]{:S(2)}) async-start(), calls=%async_computation.2 | async-start | bytes 15597568 | tf_op jit(solution)/shard_map/all_gather | solution.py:60
  54.1 204.5 %copy-start.3 = (bf16[1,64,3584]{2,1,0:T(8,128)(2,1)S(1)}, bf16[1,64,3584]{2,1,0:T(8,128)(2,1)}, u32[]{:S(2)}) copy-start(bf16[1,64,3584]{2,1,0:T(8,128)(2,1)} %param.12) | copy-start | bytes 1376260
  253.1 11.7 %copy-start.1 = (bf16[1024,7168]{1,0:T(8,128)(2,1)S(1)}, bf16[1024,7168]{1,0:T(8,128)(2,1)}, u32[]{:S(2)}) copy-start(bf16[1024,7168]{1,0:T(8,128)(2,1)} %all-gather.2.cloned.1.call-done) | copy-start | bytes 44040196
  258.6 6.1 %copy-start.4 = (bf16[1,64,3584]{2,1,0:T(8,128)(2,1)S(1)}, bf16[1,64,3584]{2,1,0:T(8,128)(2,1)}, u32[]{:S(2)}) copy-start(bf16[1,64,3584]{2,1,0:T(8,128)(2,1)} %param.13) | copy-start | bytes 1376260
Sparse Core Ops, SparseCore 0:
  69.4 183.5 all-gather.1
